TPU v7x, 256 devices: a whole 4x4x8 slice. The times are simulated.
256 devices in a mesh: gx: 8 (over x, core), gy: 8 (over z), gz: 4 (over y).
Axes of the slice: x: 4, y: 4, z: 8, core: 2. Of those that a mesh axis runs over, the one named last changes fastest.
Arguments:
- load_field: float32 [3, 128, 128, 512], P(None, 'gx', 'gy', 'gz'), may hold values from -6 to 6
- design: float32 [128, 128, 512], P('gx', 'gy', 'gz'), may hold values from 0 to 1
- solid_map: int32 [8, 8, 32], replicated, may hold values from 0 to 1, as said below
Outputs:
- displacement: float32 [3, 128, 128, 512], P(None, 'gx', 'gy', 'gz')
- sensitivity: float32 [128, 128, 512], P('gx', 'gy', 'gz')
- density: float32 [128, 128, 512], P('gx', 'gy', 'gz')
Inputs may be any that keep to these rules, and one draw needn't show every extreme that they name: Brick [i, j, k] holds the elements of rows i * 16 to (i + 1) * 16 - 1 of each dimension in turn. For i < 4, every j and every aligned run of 8 bricks along the third dimension, the run at first index i and the same run at i + 4 hold exactly 8 solid bricks together. The run solid_map[0, 0, 0:8] is all solid.
All inputs are finite; a program needn't handle non-finite values.
Results may differ from a plain program's by a relative error of at most 0.0001.
Values sent between devices are 32-bit elements; how exact they have to be, the bound alone decides.
No kernel may reach another device: no remote copies, remote signals or barrier semaphores. Data moves between devices by JAX's collectives and lax.ppermute only.
A program may use at most 64 MiB of HBM per device.

v0:
```python
import math
import jax
import jax.numpy as jnp
import numpy as np
from jax import lax
from jax.sharding import Mesh
from jax.sharding import PartitionSpec as P

BRICK = 16
ITERS = 2
GX = ("gx_0", "gx_1")
GX_GY_GZ = ("gx_0", "gx_1", "gy", "gz")
young_floor = 0.001
spring_rate = 0.05
sharpness = 8.0
threshold = 0.5
poisson = 0.3
precise = lax.Precision.HIGHEST


def with_halo(block, sides, width):
    for axis, dim in sides:
        count = lax.axis_size(axis)
        forward = [(i, i + 1) for i in range(count - 1)]
        backward = [(target, source) for source, target in forward]
        low = lax.ppermute(
            lax.slice_in_dim(block, block.shape[dim] - width, None, axis=dim), axis, forward
        )
        high = lax.ppermute(lax.slice_in_dim(block, 0, width, axis=dim), axis, backward)
        block = jnp.concatenate([low, block, high], axis=dim)
    return block


def shifted(block, axis, distance):
    devices = range(lax.axis_size(axis))
    route = [(i - distance, i) for i in devices if i - distance in devices]
    return lax.ppermute(block, axis, route)


def over_axes(value, axes):
    for axis in axes:
        value = lax.psum(value, axis)
    return value


def element_matrix():
    lame_first = poisson / ((1.0 + poisson) * (1.0 - 2.0 * poisson))
    shear_mod = 1.0 / (2.0 * (1.0 + poisson))
    elastic = np.zeros((6, 6))
    elastic[:3, :3] = lame_first
    for axis_one in range(3):
        elastic[axis_one, axis_one] += 2.0 * shear_mod
        elastic[axis_one + 3, axis_one + 3] = shear_mod
    gauss_point = 1.0 / math.sqrt(3.0)
    stiffness = np.zeros((24, 24))
    for point_x in (-gauss_point, gauss_point):
        for point_y in (-gauss_point, gauss_point):
            for point_z in (-gauss_point, gauss_point):
                strain = np.zeros((6, 24))
                for corner in range(8):
                    sign_a = 2 * (corner // 4) - 1
                    sign_b = 2 * (corner // 2 % 2) - 1
                    sign_c = 2 * (corner % 2) - 1
                    along_x = 0.25 * sign_a * (1 + sign_b * point_y) * (1 + sign_c * point_z)
                    along_y = 0.25 * (1 + sign_a * point_x) * sign_b * (1 + sign_c * point_z)
                    along_z = 0.25 * (1 + sign_a * point_x) * (1 + sign_b * point_y) * sign_c
                    column = 3 * corner
                    strain[0, column] = along_x
                    strain[1, column + 1] = along_y
                    strain[2, column + 2] = along_z
                    strain[3, column + 1] = along_z
                    strain[3, column + 2] = along_y
                    strain[4, column] = along_z
                    strain[4, column + 2] = along_x
                    strain[5, column] = along_y
                    strain[5, column + 1] = along_x
                stiffness += strain.T @ elastic @ strain * 0.125
    return jnp.asarray(stiffness, dtype=jnp.float32)


def cone_offsets():
    listed = []
    for step_x in range(-2, 3):
        for step_y in range(-2, 3):
            for step_z in range(-2, 3):
                radius = step_x * step_x + step_y * step_y + step_z * step_z
                if radius < 9:
                    listed.append((step_x, step_y, step_z, 3.0 - math.sqrt(radius)))
    return listed


def corner_values(node_values, width_x, width_y, width_z):
    pieces = []
    for corner in range(8):
        shift_a, shift_b, shift_c = (corner // 4, corner // 2 % 2, corner % 2)
        pieces.append(
            node_values[
                :,
                shift_a : shift_a + width_x,
                shift_b : shift_b + width_y,
                shift_c : shift_c + width_z,
            ]
        )
    return jnp.concatenate(pieces, 0).reshape(24, -1)


def spread_back(forces, width_x, width_y, width_z):
    forces = forces.reshape(24, width_x, width_y, width_z)
    summed = jnp.zeros((3, width_x + 1, width_y + 1, width_z + 1), jnp.float32)
    for corner in range(8):
        shift_a, shift_b, shift_c = (corner // 4, corner // 2 % 2, corner % 2)
        summed = summed + jnp.pad(
            forces[3 * corner : 3 * corner + 3],
            ((0, 0), (shift_a, 1 - shift_a), (shift_b, 1 - shift_b), (shift_c, 1 - shift_c)),
        )
    return summed


def corner_energy(stiffness, corner_vals):
    return jnp.sum(
        corner_vals
        * jnp.dot(stiffness, corner_vals, precision=precise, preferred_element_type=jnp.float32),
        0,
    )


def brick_product(stiffness, node_values, brick_moduli):
    width_x, width_y, width_z = brick_moduli.shape
    corner_vals = corner_values(node_values, width_x, width_y, width_z)
    forces = jnp.dot(
        stiffness,
        corner_vals * brick_moduli.reshape(1, -1),
        precision=precise,
        preferred_element_type=jnp.float32,
    )
    return spread_back(forces, width_x, width_y, width_z)


def body(load_field, design, solid_map):
    stiffness = element_matrix()
    offsets = cone_offsets()
    size_x, size_y, size_z = design.shape
    bricks_here = size_z // BRICK
    devices_x = lax.axis_size(GX)
    index_x = lax.axis_index(GX)
    index_y = lax.axis_index("gy")
    index_z = lax.axis_index("gz")

    def inside(dev_index, length, devices):
        coords = dev_index * length + jnp.arange(length, dtype=jnp.int32)
        return {
            step_off: ((coords + step_off >= 0) & (coords + step_off < length * devices)).astype(
                jnp.float32
            )
            for step_off in range(-2, 3)
        }

    inside_x = inside(index_x, size_x, devices_x)
    inside_y = inside(index_y, size_y, lax.axis_size("gy"))
    inside_z = inside(index_z, size_z, lax.axis_size("gz"))
    weight_sum = jnp.zeros((size_x, size_y, size_z), jnp.float32)
    for step_x, step_y, step_z, weight in offsets:
        weight_sum = weight_sum + weight * (
            inside_x[step_x][:, None, None]
            * inside_y[step_y][None, :, None]
            * inside_z[step_z][None, None, :]
        )

    def cone_sum(values):
        extended = with_halo(values, ((GX, 0), ("gy", 1), ("gz", 2)), 2)
        summed = jnp.zeros_like(values)
        for step_x, step_y, step_z, weight in offsets:
            summed = (
                summed
                + weight
                * extended[
                    2 + step_x : 2 + step_x + size_x,
                    2 + step_y : 2 + step_y + size_y,
                    2 + step_z : 2 + step_z + size_z,
                ]
            )
        return summed

    smoothed = cone_sum(design) / weight_sum
    lift_value = math.tanh(sharpness * threshold)
    scale_sum = lift_value + math.tanh(sharpness * (1.0 - threshold))
    tanh_shift = jnp.tanh(sharpness * (smoothed - threshold))
    density = (lift_value + tanh_shift) / scale_sum
    own_flags = lax.dynamic_slice(
        solid_map, (index_x, index_y, index_z * bricks_here), (1, 1, bricks_here)
    ).reshape(bricks_here)
    cell_flags = jnp.repeat(own_flags.astype(jnp.float32), BRICK)
    moduli = (young_floor + density**3 * (1.0 - young_floor)) * cell_flags

    def clamp_axis(length, devices, dev_index):
        return jnp.where(
            (jnp.arange(length + 1) == length) & (dev_index == devices - 1), 0.0, 1.0
        ).astype(jnp.float32)

    clamp_mask = (
        clamp_axis(size_x, devices_x, index_x)[:, None, None]
        * clamp_axis(size_y, lax.axis_size("gy"), index_y)[None, :, None]
        * clamp_axis(size_z, lax.axis_size("gz"), index_z)[None, None, :]
    )

    def assemble(partial_value):
        extended = with_halo(partial_value, ((GX, 1), ("gy", 2), ("gz", 3)), 1)
        for axis_one in (1, 2, 3):
            length = extended.shape[axis_one]
            lower_part = lax.slice_in_dim(extended, 0, 1, axis=axis_one) + lax.slice_in_dim(
                extended, 1, 2, axis=axis_one
            )
            middle = lax.slice_in_dim(extended, 2, length - 2, axis=axis_one)
            upper_part = lax.slice_in_dim(
                extended, length - 2, length - 1, axis=axis_one
            ) + lax.slice_in_dim(extended, length - 1, length, axis=axis_one)
            extended = jnp.concatenate([lower_part, middle, upper_part], axis_one)
        return extended * clamp_mask

    def owned_sum(left, right):
        return jnp.sum(left[:, :size_x, :size_y, :size_z] * right[:, :size_x, :size_y, :size_z])

    zero_nodes = jnp.zeros((3, size_x + 1, size_y + 1, size_z + 1), jnp.float32)

    def piece_of(node_values, offset_z):
        return lax.dynamic_slice_in_dim(node_values, offset_z, BRICK + 1, 3)

    def moduli_of(offset_z):
        return lax.dynamic_slice_in_dim(moduli, offset_z, BRICK, 2)

    def add_into(summed, offset_z, contribution):
        current = lax.dynamic_slice_in_dim(summed, offset_z, BRICK + 1, 3)
        return lax.dynamic_update_slice_in_dim(summed, current + contribution, offset_z, 3)

    def products(node_values):

        def brick_step(position, summed):
            offset_z = position * BRICK

            def brick_compute(summed):
                return add_into(
                    summed,
                    offset_z,
                    brick_product(stiffness, piece_of(node_values, offset_z), moduli_of(offset_z)),
                )

            def skip_brick(summed):
                return summed

            return lax.cond(own_flags[position] > 0, brick_compute, skip_brick, summed)

        return lax.fori_loop(0, bricks_here, brick_step, zero_nodes)

    def operate(vector):
        return assemble(products(vector)) + spring_rate * vector

    upper_z = shifted(load_field[:, :, :, :1], "gz", -1)
    extended_z = jnp.concatenate([load_field, upper_z], 3)
    upper_y = shifted(extended_z[:, :, :1, :], "gy", -1)
    extended_y = jnp.concatenate([extended_z, upper_y], 2)
    upper_x = shifted(extended_y[:, :1, :, :], GX, -1)
    loaded = jnp.concatenate([extended_y, upper_x], 1) * clamp_mask

    def two_products(residual, applied):
        return (
            over_axes(owned_sum(residual, residual), GX_GY_GZ),
            over_axes(owned_sum(residual, applied), GX_GY_GZ),
        )

    solution = zero_nodes
    residual = loaded
    applied = operate(residual)
    norm_now, product = two_products(residual, applied)
    step_size = norm_now / product
    direction, applied_dir = (residual, applied)
    for iteration in range(ITERS):
        solution = solution + step_size * direction
        residual = residual - step_size * applied_dir
        if iteration + 1 < ITERS:
            applied = operate(residual)
            norm_next, product = two_products(residual, applied)
            norm_ratio = norm_next / norm_now
            step_size = norm_next / (product - norm_ratio * norm_next / step_size)
            direction = residual + norm_ratio * direction
            applied_dir = applied + norm_ratio * applied_dir
            norm_now = norm_next

    def energy_step(position, summed):
        offset_z = position * BRICK

        def energy_compute(summed):
            corner_vals = corner_values(piece_of(solution, offset_z), size_x, size_y, BRICK)
            values = corner_energy(stiffness, corner_vals).reshape(size_x, size_y, BRICK)
            return lax.dynamic_update_slice_in_dim(summed, values, offset_z, 2)

        def skip_energy(summed):
            return summed

        return lax.cond(own_flags[position] > 0, energy_compute, skip_energy, summed)

    energy = lax.fori_loop(
        0, bricks_here, energy_step, jnp.zeros((size_x, size_y, size_z), jnp.float32)
    )
    pushed = (
        -3.0
        * (1.0 - young_floor)
        * density**2
        * cell_flags
        * energy
        * (sharpness * (1.0 - tanh_shift * tanh_shift) / scale_sum)
        / weight_sum
    )
    sensitivity = cone_sum(pushed)
    return (solution[:, :size_x, :size_y, :size_z], sensitivity, density)


def solution(mesh):
    torus = Mesh(
        mesh.devices.reshape(4, 2, mesh.shape["gy"], mesh.shape["gz"]), ("gx_0", "gx_1", "gy", "gz")
    )
    placed = (P(None, GX, "gy", "gz"), P(GX, "gy", "gz"), P())
    return jax.shard_map(
        body,
        mesh=torus,
        in_specs=placed,
        out_specs=(P(None, GX, "gy", "gz"), P(GX, "gy", "gz"), P(GX, "gy", "gz")),
        check_vma=False,
    )
```

profile of v0, /device:TPU:1, one launch (start us, length us, event | category | flops | bytes accessed | tf_op | source)
XLA Modules:
  0.0 896.5 jit_solution(13874755931423796651)
XLA Ops:
  1.4 4.5 collective-permute-start.3
  5.9 1.9 collective-permute-start.4
  7.8 1.3 collective-permute-start
  10.9 1.3 fusion.239
  12.2 8.4 collective-permute-done
  22.2 4.0 collective-permute-start.5
  27.7 3.0 collective-permute-done.6
  30.9 2.2 collective-permute-start.7
  34.4 3.4 collective-permute-start.2
  37.8 3.5 collective-permute-done.8
  41.9 4.7 fusion.62
  48.3 46.9 %while.51 = (s32[]{:T(128)}, f32[3,17,17,129]{3,2,1,0:T(8,128)}, s32[8]{0:T(128)}, f32[3,17,17,129]{3,2,1,0:T(8,128)S(1)}, f32[16,16,128]{2,1,0:T(8,128)}, /*index=5*/s32[]{:T(128)}, s32[1]{0:T(128)}) while((s32[]{:T(128)}, f32[3,17,17,129]{3,2,1,0:T(8,128)}, s32[8]{0:T(128)}, f32[3,17,17,129]{3,2,1,0:T(8,128)S(1)}, ...), condition=%wide.region_8.9_spmd.clone, body=%wide.region_5.8_spmd.sunk.clone.sunk | while | flops 28527780 | bytes 7407486 | solution.py:252
  56.1 31.4 %conditional.12 = (f32[3,17,17,129]{3,2,1,0:T(8,128)}) conditional(s32[]{:T(128)} %bitcast.33, f32[3,17,17,129]{3,2,1,0:T(8,128)} %get-tuple-element.762, (s32[]{:T(128)}, f32[3,17,17,129]{3,2,1,0:T(8,128)}, f32[3,17,17,129]{3,2,1,0:T(8,128)S(1)}, f32[16,16,128]{2,1,0:T(8,128)}) %tuple.222), branch_computations={%region_6.6_spmd, %region_7.7_spmd.clone} | conditional | flops 28527776 | bytes 7407351 | solution.py:250
  63.5 3.8 reshape.959
  73.4 2.6 add_add_fusion
  76.0 11.5 %dynamic_update_slice.12 = f32[3,17,17,129]{3,2,1,0:T(8,128)} dynamic-update-slice(f32[3,17,17,129]{3,2,1,0:T(8,128)} %get-tuple-element.486, f32[3,17,17,17]{3,2,1,0:T(8,128)S(1)} %add_add_fusion, s32[]{:T(128)} %constant.166.clone.1, s32[]{:T(128)} %constant.166.clone.1, s32[]{:T(128)} %constant.166.clone.1, s32[]{:T(128)S(6)} %select_n.81) | dynamic-update-slice | bytes 117916 | tf_op jit(solution)/shard_map/while/body/eval_jaxpr/cond/branch_1_fun/dynamic_update_slice | solution.py:233
  96.2 163.3 %collective-permute-start.9 = (f32[3,1,17,129]{3,2,1,0:T(8,128)S(1)}, f32[3,1,17,129]{3,2,1,0:T(8,128)S(1)}, u32[]{:S(2)}, u32[]{:S(2)}) collective-permute-start(f32[3,1,17,129]{3,2,1,0:T(8,128)S(1)} %get-tuple-element.599), channel_id=1, source_target_pairs={{0,32},{32,64},{64,96},{96,128},{128,160},{160,192},{192,224},{1,3... | collective-permute-start | bytes 78956 | tf_op jit(solution)/shard_map/ppermute | solution.py:26
  259.4 54.8 %collective-permute-start.10 = (f32[3,1,17,129]{3,2,1,0:T(8,128)S(1)}, f32[3,1,17,129]{3,2,1,0:T(8,128)S(1)}, u32[]{:S(2)}, u32[]{:S(2)}) collective-permute-start(f32[3,1,17,129]{3,2,1,0:T(8,128)S(1)} %get-tuple-element.600), channel_id=1, source_target_pairs={{32,0},{64,32},{96,64},{128,96},{160,128},{192,160},{224,192},{33,... | collective-permute-start | bytes 78956 | tf_op jit(solution)/shard_map/ppermute | solution.py:29
  314.2 1.6 copy.46
  316.0 1.3 collective-permute-start.11
  319.1 4.4 collective-permute-done.12
  324.7 1.6 copy.48
  326.3 11.0 %collective-permute-start.13 = (f32[3,19,19,1]{2,1,3,0:T(8,128)S(1)}, f32[3,19,19,1]{2,1,3,0:T(8,128)S(1)}, u32[]{:S(2)}, u32[]{:S(2)}) collective-permute-start(f32[3,19,19,1]{2,1,3,0:T(8,128)S(1)} %copy.48), channel_id=1, source_target_pairs={{0,1},{1,2},{2,3},{4,5},{5,6},{6,7},{8,9},{9,10},{10,11},{12,13},{... | collective-permute-start | bytes 13004 | tf_op jit(solution)/shard_map/ppermute | solution.py:26
  339.7 1.5 copy.51
  341.7 1.8 collective-permute-done.14
  343.5 2.1 copy.52
  345.5 1.8 pad_maximum_fusion.1
  351.6 6.7 all-reduce.21
  358.3 7.5 all-reduce.23
  365.7 13.1 %all-reduce.17 = (f32[]{:T(128)}, f32[]{:T(128)}) all-reduce(f32[]{:T(128)} %get-tuple-element.554, f32[]{:T(128)} %get-tuple-element.555), channel_id=1, replica_groups=mesh['gx_0'=4,'gx_1'=2,'gy'=8,'gz'=4] {'gy'}, use_global_device_ids=true, to_apply=%region_3.4 | all-reduce | flops 2 | bytes 16 | tf_op jit(solution)/shard_map/psum | solution.py:42
  378.8 6.7 all-reduce.19
  389.3 46.8 %while.52 = (s32[]{:T(128)}, f32[3,17,17,129]{3,2,1,0:T(8,128)}, s32[8]{0:T(128)}, f32[3,17,17,129]{3,2,1,0:T(8,128)S(1)}, f32[16,16,128]{2,1,0:T(8,128)}, /*index=5*/s32[]{:T(128)}, s32[1]{0:T(128)}) while((s32[]{:T(128)}, f32[3,17,17,129]{3,2,1,0:T(8,128)}, s32[8]{0:T(128)}, f32[3,17,17,129]{3,2,1,0:T(8,128)S(1)}, ...), condition=%wide.region_22.23_spmd.clone, body=%wide.region_19.22_spmd.sunk.clone.sunk | while | flops 28527780 | bytes 7407486 | solution.py:252
  397.1 31.3 %conditional.13 = (f32[3,17,17,129]{3,2,1,0:T(8,128)}) conditional(s32[]{:T(128)} %bitcast.34, f32[3,17,17,129]{3,2,1,0:T(8,128)} %get-tuple-element.783, (s32[]{:T(128)}, f32[3,17,17,129]{3,2,1,0:T(8,128)}, f32[3,17,17,129]{3,2,1,0:T(8,128)S(1)}, f32[16,16,128]{2,1,0:T(8,128)}) %tuple.224), branch_computations={%region_20.20_spmd, %region_21.21_spmd.clone} | conditional | flops 28527776 | bytes 7407351 | solution.py:250
  404.5 3.8 reshape.960
  414.4 2.6 add_add_fusion.1
  416.9 11.5 %dynamic_update_slice.13 = f32[3,17,17,129]{3,2,1,0:T(8,128)} dynamic-update-slice(f32[3,17,17,129]{3,2,1,0:T(8,128)} %get-tuple-element.494, f32[3,17,17,17]{3,2,1,0:T(8,128)S(1)} %add_add_fusion.1, s32[]{:T(128)} %constant.174.clone.1, s32[]{:T(128)} %constant.174.clone.1, s32[]{:T(128)} %constant.174.clone.1, s32[]{:T(128)S(6)} %select_n.83) | dynamic-update-slice | bytes 117916 | tf_op jit(solution)/shard_map/while/body/eval_jaxpr/cond/branch_1_fun/dynamic_update_slice | solution.py:233
  437.1 165.1 %collective-permute-start.15 = (f32[3,1,17,129]{3,2,1,0:T(8,128)S(1)}, f32[3,1,17,129]{3,2,1,0:T(8,128)S(1)}, u32[]{:S(2)}, u32[]{:S(2)}) collective-permute-start(f32[3,1,17,129]{3,2,1,0:T(8,128)S(1)} %get-tuple-element.593), channel_id=1, source_target_pairs={{0,32},{32,64},{64,96},{96,128},{128,160},{160,192},{192,224},{1,3... | collective-permute-start | bytes 78956 | tf_op jit(solution)/shard_map/ppermute | solution.py:26
  602.2 56.5 %collective-permute-start.16 = (f32[3,1,17,129]{3,2,1,0:T(8,128)S(1)}, f32[3,1,17,129]{3,2,1,0:T(8,128)S(1)}, u32[]{:S(2)}, u32[]{:S(2)}) collective-permute-start(f32[3,1,17,129]{3,2,1,0:T(8,128)S(1)} %get-tuple-element.594), channel_id=1, source_target_pairs={{32,0},{64,32},{96,64},{128,96},{160,128},{192,160},{224,192},{33,... | collective-permute-start | bytes 78956 | tf_op jit(solution)/shard_map/ppermute | solution.py:29
  658.7 1.6 copy.54
  660.5 1.3 collective-permute-start.17
  663.6 4.4 collective-permute-done.18
  669.2 1.6 copy.56
  670.8 5.1 collective-permute-start.19
  678.3 1.6 slice.1586
  679.9 1.5 copy.59
  682.0 2.1 copy.60
  684.1 1.8 pad_maximum_fusion.3
  689.0 7.7 all-reduce.20
  696.7 6.8 all-reduce.22
  703.6 12.5 %all-reduce.16 = (f32[]{:T(128)}, f32[]{:T(128)}) all-reduce(f32[]{:T(128)} %get-tuple-element.552, f32[]{:T(128)} %get-tuple-element.553), channel_id=1, replica_groups=mesh['gx_0'=4,'gx_1'=2,'gy'=8,'gz'=4] {'gy'}, use_global_device_ids=true, to_apply=%region_17.18 | all-reduce | flops 2 | bytes 16 | tf_op jit(solution)/shard_map/psum | solution.py:42
  716.1 8.9 all-reduce.18
  729.7 1.4 multiply_add_fusion
  731.3 29.9 %while.53 = (s32[]{:T(128)}, f32[16,16,128]{2,1,0:T(8,128)S(1)}, s32[8]{0:T(128)}, f32[3,17,17,129]{3,2,1,0:T(8,128)S(1)}, s32[]{:T(128)}, /*index=5*/s32[1]{0:T(128)}) while((s32[]{:T(128)}, f32[16,16,128]{2,1,0:T(8,128)S(1)}, s32[8]{0:T(128)}, f32[3,17,17,129]{3,2,1,0:T(8,128)S(1)}, s32[]{:T(128)}, ...), condition=%wide.region_32.33_spmd.clone, body=%wide.region_28.32_spmd.sunk.clone.sunk | while | flops 28504076 | bytes 4812342 | solution.py:301
  739.1 14.4 %conditional.14 = (f32[16,16,128]{2,1,0:T(8,128)S(1)}) conditional(s32[]{:T(128)} %bitcast.35, f32[16,16,128]{2,1,0:T(8,128)S(1)} %get-tuple-element.803, (s32[]{:T(128)}, f32[3,17,17,129]{3,2,1,0:T(8,128)S(1)}, f32[16,16,128]{2,1,0:T(8,128)S(1)}) %tuple.226), branch_computations={%region_29.29_spmd, %region_30.31_spmd.clone} | conditional | flops 28504072 | bytes 4812223 | solution.py:299
  746.6 3.8 reshape.961
  751.0 2.5 dynamic_update_slice.14
  761.5 1.7 fusion.65
  763.2 81.2 %collective-permute-start.21 = (f32[2,16,128]{2,1,0:T(8,128)S(1)}, f32[2,16,128]{2,1,0:T(8,128)S(1)}, u32[]{:S(2)}, u32[]{:S(2)}) collective-permute-start(f32[2,16,128]{2,1,0:T(8,128)S(1)} %get-tuple-element.615), channel_id=1, source_target_pairs={{0,32},{32,64},{64,96},{96,128},{128,160},{160,192},{192,224},{1,3... | collective-permute-start | bytes 49160 | tf_op jit(solution)/shard_map/ppermute | solution.py:26
  844.4 26.2 %collective-permute-start.22 = (f32[2,16,128]{2,1,0:T(8,128)S(1)}, f32[2,16,128]{2,1,0:T(8,128)S(1)}, u32[]{:S(2)}, u32[]{:S(2)}) collective-permute-start(f32[2,16,128]{2,1,0:T(8,128)S(1)} %get-tuple-element.616), channel_id=1, source_target_pairs={{32,0},{64,32},{96,64},{128,96},{160,128},{192,160},{224,192},{33,... | collective-permute-start | bytes 49160 | tf_op jit(solution)/shard_map/ppermute | solution.py:29
  874.9 2.4 collective-permute-done.24
  877.5 5.7 collective-permute-start.25
  884.5 4.0 collective-permute-done.25
  888.6 4.3 collective-permute-done.26
  893.2 2.9 fusion.189
  (338 shorter events, 103.8 us)
Async XLA Ops:
  1.4 20.7 %collective-permute-start.3 = (f32[2,16,128]{2,1,0:T(8,128)S(1)}, f32[2,16,128]{2,1,0:T(8,128)S(1)}, u32[]{:S(2)}, u32[]{:S(2)}) collective-permute-start(f32[2,16,128]{2,1,0:T(8,128)S(1)} %get-tuple-element.621), channel_id=1, source_target_pairs={{0,32},{32,64},{64,96},{96,128},{128,160},{160,192},{192,224},{1,3... | collective-permute-start | bytes 49160 | tf_op jit(solution)/shard_map/ppermute | solution.py:26
  5.9 16.3 %collective-permute-start.4 = (f32[2,16,128]{2,1,0:T(8,128)S(1)}, f32[2,16,128]{2,1,0:T(8,128)S(1)}, u32[]{:S(2)}, u32[]{:S(2)}) collective-permute-start(f32[2,16,128]{2,1,0:T(8,128)S(1)} %get-tuple-element.620), channel_id=1, source_target_pairs={{32,0},{64,32},{96,64},{128,96},{160,128},{192,160},{224,192},{33,... | collective-permute-start | bytes 49160 | tf_op jit(solution)/shard_map/ppermute | solution.py:29
  7.8 12.9 %collective-permute-start = (f32[3,16,16,1]{3,2,1,0:T(8,128)}, f32[3,16,16,1]{3,2,1,0:T(8,128)S(1)}, u32[]{:S(2)}, u32[]{:S(2)}) collective-permute-start(f32[3,16,16,1]{3,2,1,0:T(8,128)} %bitcast.36), channel_id=1, source_target_pairs={{1,0},{2,1},{3,2},{5,4},{6,5},{7,6},{9,8},{10,9},{11,10},{13,12},{... | collective-permute-start | bytes 9224 | tf_op jit(solution)/shard_map/ppermute | solution.py:37
  9.2 32.5 %copy-start.59 = (f32[128]{0:T(128)}, f32[128]{0:T(128)S(1)}, u32[]{:S(2)}) copy-start(f32[128]{0:T(128)S(1)} %get-tuple-element.663) | copy-start | bytes 1540
  9.2 32.5 %copy-start.61 = (f32[128]{0:T(128)}, f32[128]{0:T(128)S(1)}, u32[]{:S(2)}) copy-start(f32[128]{0:T(128)S(1)} %get-tuple-element.664) | copy-start | bytes 1540
  9.2 32.4 %copy-start.63 = (f32[128]{0:T(128)}, f32[128]{0:T(128)S(1)}, u32[]{:S(2)}) copy-start(f32[128]{0:T(128)S(1)} %get-tuple-element.665) | copy-start | bytes 1540
  9.2 32.4 %copy-start.65 = (f32[128]{0:T(128)}, f32[128]{0:T(128)S(1)}, u32[]{:S(2)}) copy-start(f32[128]{0:T(128)S(1)} %get-tuple-element.666) | copy-start | bytes 1540
  10.6 36.0 %copy-start.7 = (f32[17,17,129]{2,1,0:T(8,128)}, f32[17,17,129]{2,1,0:T(8,128)S(1)}, u32[]{:S(2)}) copy-start(f32[17,17,129]{2,1,0:T(8,128)S(1)} %broadcast_multiply_fusion) | copy-start | bytes 447376
  10.7 31.0 %copy-start.21 = (f32[16,16]{1,0:T(8,128)}, f32[16,16]{1,0:T(8,128)S(1)}, u32[]{:S(2)}) copy-start(f32[16,16]{1,0:T(8,128)S(1)} %get-tuple-element.632) | copy-start | bytes 3076
  10.7 31.0 %copy-start.23 = (f32[16,16]{1,0:T(8,128)}, f32[16,16]{1,0:T(8,128)S(1)}, u32[]{:S(2)}) copy-start(f32[16,16]{1,0:T(8,128)S(1)} %get-tuple-element.633) | copy-start | bytes 3076
  10.7 31.0 %copy-start.25 = (f32[16,16]{1,0:T(8,128)}, f32[16,16]{1,0:T(8,128)S(1)}, u32[]{:S(2)}) copy-start(f32[16,16]{1,0:T(8,128)S(1)} %get-tuple-element.634) | copy-start | bytes 3076
  10.7 31.0 %copy-start.27 = (f32[16,16]{1,0:T(8,128)}, f32[16,16]{1,0:T(8,128)S(1)}, u32[]{:S(2)}) copy-start(f32[16,16]{1,0:T(8,128)S(1)} %get-tuple-element.635) | copy-start | bytes 3076
  10.7 31.0 %copy-start.29 = (f32[16,16]{1,0:T(8,128)}, f32[16,16]{1,0:T(8,128)S(1)}, u32[]{:S(2)}) copy-start(f32[16,16]{1,0:T(8,128)S(1)} %get-tuple-element.636) | copy-start | bytes 3076
  10.8 31.0 %copy-start.31 = (f32[16,16]{1,0:T(8,128)}, f32[16,16]{1,0:T(8,128)S(1)}, u32[]{:S(2)}) copy-start(f32[16,16]{1,0:T(8,128)S(1)} %get-tuple-element.637) | copy-start | bytes 3076
  10.8 31.0 %copy-start.33 = (f32[16,16]{1,0:T(8,128)}, f32[16,16]{1,0:T(8,128)S(1)}, u32[]{:S(2)}) copy-start(f32[16,16]{1,0:T(8,128)S(1)} %get-tuple-element.638) | copy-start | bytes 3076
  10.8 31.0 %copy-start.35 = (f32[16,16]{1,0:T(8,128)}, f32[16,16]{1,0:T(8,128)S(1)}, u32[]{:S(2)}) copy-start(f32[16,16]{1,0:T(8,128)S(1)} %get-tuple-element.639) | copy-start | bytes 3076
  10.8 31.0 %copy-start.37 = (f32[16,16]{1,0:T(8,128)}, f32[16,16]{1,0:T(8,128)S(1)}, u32[]{:S(2)}) copy-start(f32[16,16]{1,0:T(8,128)S(1)} %get-tuple-element.640) | copy-start | bytes 3076
  10.8 31.0 %copy-start.39 = (f32[16,16]{1,0:T(8,128)}, f32[16,16]{1,0:T(8,128)S(1)}, u32[]{:S(2)}) copy-start(f32[16,16]{1,0:T(8,128)S(1)} %get-tuple-element.641) | copy-start | bytes 3076
  10.8 31.0 %copy-start.41 = (f32[16,16]{1,0:T(8,128)}, f32[16,16]{1,0:T(8,128)S(1)}, u32[]{:S(2)}) copy-start(f32[16,16]{1,0:T(8,128)S(1)} %get-tuple-element.642) | copy-start | bytes 3076
  10.8 31.0 %copy-start.43 = (f32[16,16]{1,0:T(8,128)}, f32[16,16]{1,0:T(8,128)S(1)}, u32[]{:S(2)}) copy-start(f32[16,16]{1,0:T(8,128)S(1)} %get-tuple-element.643) | copy-start | bytes 3076
  10.8 31.0 %copy-start.45 = (f32[16,16]{1,0:T(8,128)}, f32[16,16]{1,0:T(8,128)S(1)}, u32[]{:S(2)}) copy-start(f32[16,16]{1,0:T(8,128)S(1)} %get-tuple-element.644) | copy-start | bytes 3076
  10.8 31.0 %copy-start.47 = (f32[16,16]{1,0:T(8,128)}, f32[16,16]{1,0:T(8,128)S(1)}, u32[]{:S(2)}) copy-start(f32[16,16]{1,0:T(8,128)S(1)} %get-tuple-element.645) | copy-start | bytes 3076
  10.8 31.0 %copy-start.49 = (f32[16,16]{1,0:T(8,128)}, f32[16,16]{1,0:T(8,128)S(1)}, u32[]{:S(2)}) copy-start(f32[16,16]{1,0:T(8,128)S(1)} %get-tuple-element.646) | copy-start | bytes 3076
  10.9 31.0 %copy-start.51 = (f32[16,16]{1,0:T(8,128)}, f32[16,16]{1,0:T(8,128)S(1)}, u32[]{:S(2)}) copy-start(f32[16,16]{1,0:T(8,128)S(1)} %get-tuple-element.647) | copy-start | bytes 3076
  10.9 31.0 %copy-start.53 = (f32[16,16]{1,0:T(8,128)}, f32[16,16]{1,0:T(8,128)S(1)}, u32[]{:S(2)}) copy-start(f32[16,16]{1,0:T(8,128)S(1)} %get-tuple-element.648) | copy-start | bytes 3076
  10.9 31.0 %copy-start.55 = (f32[16,16]{1,0:T(8,128)}, f32[16,16]{1,0:T(8,128)S(1)}, u32[]{:S(2)}) copy-start(f32[16,16]{1,0:T(8,128)S(1)} %get-tuple-element.649) | copy-start | bytes 3076
  10.9 31.0 %copy-start.57 = (f32[16,16]{1,0:T(8,128)}, f32[16,16]{1,0:T(8,128)S(1)}, u32[]{:S(2)}) copy-start(f32[16,16]{1,0:T(8,128)S(1)} %get-tuple-element.650) | copy-start | bytes 3076
  20.8 6.9 collective-permute-start.1
  22.2 5.5 collective-permute-start.5
  26.2 4.5 collective-permute-start.6
  30.9 6.9 collective-permute-start.7
  33.1 8.2 collective-permute-start.8
  34.4 12.1 %collective-permute-start.2 = (f32[3,1,17,129]{3,2,1,0:T(8,128)S(1)}, f32[3,1,17,129]{3,2,1,0:T(8,128)S(1)}, u32[]{:S(2)}, u32[]{:S(2)}) collective-permute-start(f32[3,1,17,129]{3,2,1,0:T(8,128)S(1)} %pad_maximum_fusion.25), channel_id=1, source_target_pairs={{32,0},{64,32},{96,64},{128,96},{160,128},{192,160},{224,192},{33,... | collective-permute-start | bytes 78956 | tf_op jit(solution)/shard_map/ppermute | solution.py:37
  96.2 219.7 %collective-permute-start.9 = (f32[3,1,17,129]{3,2,1,0:T(8,128)S(1)}, f32[3,1,17,129]{3,2,1,0:T(8,128)S(1)}, u32[]{:S(2)}, u32[]{:S(2)}) collective-permute-start(f32[3,1,17,129]{3,2,1,0:T(8,128)S(1)} %get-tuple-element.599), channel_id=1, source_target_pairs={{0,32},{32,64},{64,96},{96,128},{128,160},{160,192},{192,224},{1,3... | collective-permute-start | bytes 78956 | tf_op jit(solution)/shard_map/ppermute | solution.py:26
  259.4 56.5 %collective-permute-start.10 = (f32[3,1,17,129]{3,2,1,0:T(8,128)S(1)}, f32[3,1,17,129]{3,2,1,0:T(8,128)S(1)}, u32[]{:S(2)}, u32[]{:S(2)}) collective-permute-start(f32[3,1,17,129]{3,2,1,0:T(8,128)S(1)} %get-tuple-element.600), channel_id=1, source_target_pairs={{32,0},{64,32},{96,64},{128,96},{160,128},{192,160},{224,192},{33,... | collective-permute-start | bytes 78956 | tf_op jit(solution)/shard_map/ppermute | solution.py:29
  316.0 3.1 collective-permute-start.11
  317.3 6.2 collective-permute-start.12
  326.3 14.9 %collective-permute-start.13 = (f32[3,19,19,1]{2,1,3,0:T(8,128)S(1)}, f32[3,19,19,1]{2,1,3,0:T(8,128)S(1)}, u32[]{:S(2)}, u32[]{:S(2)}) collective-permute-start(f32[3,19,19,1]{2,1,3,0:T(8,128)S(1)} %copy.48), channel_id=1, source_target_pairs={{0,1},{1,2},{2,3},{4,5},{5,6},{6,7},{8,9},{9,10},{10,11},{12,13},{... | collective-permute-start | bytes 13004 | tf_op jit(solution)/shard_map/ppermute | solution.py:26
  338.5 5.0 collective-permute-start.14
  350.6 37.6 %copy-start.3 = (f32[3,17,17,129]{3,2,1,0:T(8,128)}, f32[3,17,17,129]{3,2,1,0:T(8,128)S(1)}, u32[]{:S(2)}) copy-start(f32[3,17,17,129]{3,2,1,0:T(8,128)S(1)} %fusion.6) | copy-start | bytes 1342120
  437.1 223.2 %collective-permute-start.15 = (f32[3,1,17,129]{3,2,1,0:T(8,128)S(1)}, f32[3,1,17,129]{3,2,1,0:T(8,128)S(1)}, u32[]{:S(2)}, u32[]{:S(2)}) collective-permute-start(f32[3,1,17,129]{3,2,1,0:T(8,128)S(1)} %get-tuple-element.593), channel_id=1, source_target_pairs={{0,32},{32,64},{64,96},{96,128},{128,160},{160,192},{192,224},{1,3... | collective-permute-start | bytes 78956 | tf_op jit(solution)/shard_map/ppermute | solution.py:26
  602.2 58.2 %collective-permute-start.16 = (f32[3,1,17,129]{3,2,1,0:T(8,128)S(1)}, f32[3,1,17,129]{3,2,1,0:T(8,128)S(1)}, u32[]{:S(2)}, u32[]{:S(2)}) collective-permute-start(f32[3,1,17,129]{3,2,1,0:T(8,128)S(1)} %get-tuple-element.594), channel_id=1, source_target_pairs={{32,0},{64,32},{96,64},{128,96},{160,128},{192,160},{224,192},{33,... | collective-permute-start | bytes 78956 | tf_op jit(solution)/shard_map/ppermute | solution.py:29
  660.5 3.1 collective-permute-start.17
  661.8 6.2 collective-permute-start.18
  670.8 10.6 %collective-permute-start.19 = (f32[3,19,19,1]{2,1,3,0:T(8,128)S(1)}, f32[3,19,19,1]{2,1,3,0:T(8,128)S(1)}, u32[]{:S(2)}, u32[]{:S(2)}) collective-permute-start(f32[3,19,19,1]{2,1,3,0:T(8,128)S(1)} %copy.56), channel_id=1, source_target_pairs={{0,1},{1,2},{2,3},{4,5},{5,6},{6,7},{8,9},{9,10},{10,11},{12,13},{... | collective-permute-start | bytes 13004 | tf_op jit(solution)/shard_map/ppermute | solution.py:26
  677.0 5.0 collective-permute-start.20
  687.6 42.1 %copy-start.2 = (f32[3,16,16,129]{3,2,1,0:T(8,128)S(1)}, f32[3,16,16,129]{3,2,1,0:T(8,128)}, u32[]{:S(2)}) copy-start(f32[3,16,16,129]{3,2,1,0:T(8,128)} %copy-done) | copy-start | bytes 1188868
  687.6 42.1 %copy-start.4 = (f32[3,17,17,129]{3,2,1,0:T(8,128)S(1)}, f32[3,17,17,129]{3,2,1,0:T(8,128)}, u32[]{:S(2)}) copy-start(f32[3,17,17,129]{3,2,1,0:T(8,128)} %copy-done.3) | copy-start | bytes 1342120
  687.6 42.1 %copy-start.13 = (f32[3,1,17,129]{3,2,1,0:T(8,128)S(1)}, f32[3,1,17,129]{3,2,1,0:T(8,128)}, u32[]{:S(2)}) copy-start(f32[3,1,17,129]{3,2,1,0:T(8,128)} %copy-done.11) | copy-start | bytes 78952
  731.1 30.2 %copy-start.15 = (f32[16,16,128]{2,1,0:T(8,128)S(1)}, f32[16,16,128]{2,1,0:T(8,128)}, u32[]{:S(2)}) copy-start(f32[16,16,128]{2,1,0:T(8,128)} %get-tuple-element.557) | copy-start | bytes 393220
  731.1 30.2 %copy-start.16 = (f32[16,16,128]{2,1,0:T(8,128)S(1)}, f32[16,16,128]{2,1,0:T(8,128)}, u32[]{:S(2)}) copy-start(f32[16,16,128]{2,1,0:T(8,128)} %get-tuple-element.558) | copy-start | bytes 393220
  731.1 30.2 %copy-start.22 = (f32[16,16]{1,0:T(8,128)S(1)}, f32[16,16]{1,0:T(8,128)}, u32[]{:S(2)}) copy-start(f32[16,16]{1,0:T(8,128)} %copy-done.21) | copy-start | bytes 3076
  731.1 30.2 %copy-start.24 = (f32[16,16]{1,0:T(8,128)S(1)}, f32[16,16]{1,0:T(8,128)}, u32[]{:S(2)}) copy-start(f32[16,16]{1,0:T(8,128)} %copy-done.23) | copy-start | bytes 3076
  731.1 30.2 %copy-start.26 = (f32[16,16]{1,0:T(8,128)S(1)}, f32[16,16]{1,0:T(8,128)}, u32[]{:S(2)}) copy-start(f32[16,16]{1,0:T(8,128)} %copy-done.25) | copy-start | bytes 3076
  731.1 30.2 %copy-start.28 = (f32[16,16]{1,0:T(8,128)S(1)}, f32[16,16]{1,0:T(8,128)}, u32[]{:S(2)}) copy-start(f32[16,16]{1,0:T(8,128)} %copy-done.27) | copy-start | bytes 3076
  731.1 30.2 %copy-start.30 = (f32[16,16]{1,0:T(8,128)S(1)}, f32[16,16]{1,0:T(8,128)}, u32[]{:S(2)}) copy-start(f32[16,16]{1,0:T(8,128)} %copy-done.29) | copy-start | bytes 3076
  731.2 30.2 %copy-start.32 = (f32[16,16]{1,0:T(8,128)S(1)}, f32[16,16]{1,0:T(8,128)}, u32[]{:S(2)}) copy-start(f32[16,16]{1,0:T(8,128)} %copy-done.31) | copy-start | bytes 3076
  731.2 30.2 %copy-start.34 = (f32[16,16]{1,0:T(8,128)S(1)}, f32[16,16]{1,0:T(8,128)}, u32[]{:S(2)}) copy-start(f32[16,16]{1,0:T(8,128)} %copy-done.33) | copy-start | bytes 3076
  763.2 107.4 %collective-permute-start.21 = (f32[2,16,128]{2,1,0:T(8,128)S(1)}, f32[2,16,128]{2,1,0:T(8,128)S(1)}, u32[]{:S(2)}, u32[]{:S(2)}) collective-permute-start(f32[2,16,128]{2,1,0:T(8,128)S(1)} %get-tuple-element.615), channel_id=1, source_target_pairs={{0,32},{32,64},{64,96},{96,128},{128,160},{160,192},{192,224},{1,3... | collective-permute-start | bytes 49160 | tf_op jit(solution)/shard_map/ppermute | solution.py:26
  844.4 27.1 %collective-permute-start.22 = (f32[2,16,128]{2,1,0:T(8,128)S(1)}, f32[2,16,128]{2,1,0:T(8,128)S(1)}, u32[]{:S(2)}, u32[]{:S(2)}) collective-permute-start(f32[2,16,128]{2,1,0:T(8,128)S(1)} %get-tuple-element.616), channel_id=1, source_target_pairs={{32,0},{64,32},{96,64},{128,96},{160,128},{192,160},{224,192},{33,... | collective-permute-start | bytes 49160 | tf_op jit(solution)/shard_map/ppermute | solution.py:29
  871.5 3.4 collective-permute-start.23
  872.8 4.5 collective-permute-start.24
  877.5 11.1 %collective-permute-start.25 = (f32[20,20,2]{2,1,0:T(8,128)S(1)}, f32[20,20,2]{2,1,0:T(8,128)S(1)}, u32[]{:S(2)}, u32[]{:S(2)}) collective-permute-start(f32[20,20,2]{2,1,0:T(8,128)S(1)} %get-tuple-element.601), channel_id=1, source_target_pairs={{0,1},{1,2},{2,3},{4,5},{5,6},{6,7},{8,9},{9,10},{10,11},{12,13},{... | collective-permute-start | bytes 9608 | tf_op jit(solution)/shard_map/ppermute | solution.py:26
  883.2 9.7 %collective-permute-start.26 = (f32[20,20,2]{2,1,0:T(8,128)S(1)}, f32[20,20,2]{2,1,0:T(8,128)S(1)}, u32[]{:S(2)}, u32[]{:S(2)}) collective-permute-start(f32[20,20,2]{2,1,0:T(8,128)S(1)} %get-tuple-element.602), channel_id=1, source_target_pairs={{1,0},{2,1},{3,2},{5,4},{6,5},{7,6},{9,8},{10,9},{11,10},{13,12},{... | collective-permute-start | bytes 9608 | tf_op jit(solution)/shard_map/ppermute | solution.py:29
  (32 other events, 595.2 us)
where the time goes:
time: 908 us; the launch traced here: 897 us
  starting transfers between devices  602 us (66%)
  local copies, waits for them, and re-layouts  131 us (14%)
  blocking collectives  69.8 us (8%)
  waiting for transfers between devices  38.3 us (4%)
  other arithmetic  28.5 us (3%)
  loops' own time  16.8 us (2%)
    ppermute x12, starting transfers between devices, with_halo(): lax.ppermute(lax.slice_in_dim(block, block.shape[dim] - width, None, axis...  446 us
    ppermute x12, starting transfers between devices, with_halo(): lax.ppermute(lax.slice_in_dim(block, 0, width, axis=dim), axis, backward)  150 us
    psum x8, blocking collectives, over_axes(): value = lax.psum(value, axis)  69.8 us
    ppermute x12, waiting for transfers between devices, with_halo(): lax.ppermute(lax.slice_in_dim(block, 0, width, axis=dim), axis, backward)  24.8 us
    dynamic_update_slice x2, local copies, waits for them, and re-layouts, add_into(): lax.dynamic_update_slice_in_dim(summed, current + contribution, offset_z, 3)  22.9 us
    dynamic_slice x16, local copies, waits for them, and re-layouts, brick_step(): return lax.cond(own_flags[position] > 0, brick_compute, skip_brick, summed)  20.1 us
    cond x27, local copies, waits for them, and re-layouts  19.4 us
  transfers between devices with their start and end apart: 27, of which 13 were waited for; matrix products, arithmetic and copies ran while one was open for 2% of the time, Pallas kernels for 0%

commit v1 on v0

--- a/solution.py
+++ b/solution.py
@@ -39,7 +39,7 @@
 
 def over_axes(value, axes):
     for axis in axes:
-        value = lax.psum(value, axis)
+        value = jnp.sum(lax.all_gather(value, axis), axis=0)
     return value
 
 

time: 908 us -> 946 us (1.042)
  local copies, waits for them, and re-layouts: 131 us -> 154 us
  starting transfers between devices: 602 us -> 613 us
  other arithmetic: 28.5 us -> 38.4 us
    psum x8 -> x0, blocking collectives: 69.8 us -> none  [over_axes(): value = lax.psum(value, axis)]
    unnamed x0 -> x8, blocking collectives: none -> 64.3 us
    unnamed x135 -> x179, local copies, waits for them, and re-layouts: 3.45 us -> 27.2 us
    ppermute x12, starting transfers between devices: 446 us -> 457 us  [with_halo(): lax.ppermute(lax.slice_in_dim(block, block.shape[dim] - width, None, axis...]
    reduce_sum x0 -> x16, other arithmetic: none -> 9.91 us  [over_axes(): value = jnp.sum(lax.all_gather(value, axis), axis=0)]
  transfers between devices with their start and end apart: 27 -> 27, of which waited for: 13 -> 12; matrix products, arithmetic and copies ran while one was open for 2% -> 2% of each run, Pallas kernels for 0% -> 0%
where the time goes in v1:
time: 946 us; the launch traced here: 934 us
  starting transfers between devices  613 us (65%)
  local copies, waits for them, and re-layouts  154 us (16%)
  blocking collectives  64.3 us (7%)
  other arithmetic  38.4 us (4%)
  waiting for transfers between devices  37.6 us (4%)
  loops' own time  16.8 us (2%)
    ppermute x12, starting transfers between devices, with_halo(): lax.ppermute(lax.slice_in_dim(block, block.shape[dim] - width, None, axis...  457 us
    ppermute x12, starting transfers between devices, with_halo(): lax.ppermute(lax.slice_in_dim(block, 0, width, axis=dim), axis, backward)  150 us
    unnamed x8, blocking collectives  64.3 us
    unnamed x179, local copies, waits for them, and re-layouts  27.2 us
    ppermute x12, waiting for transfers between devices, with_halo(): lax.ppermute(lax.slice_in_dim(block, 0, width, axis=dim), axis, backward)  24 us
    dynamic_update_slice x2, local copies, waits for them, and re-layouts, add_into(): lax.dynamic_update_slice_in_dim(summed, current + contribution, offset_z, 3)  22.9 us
    cond x27, local copies, waits for them, and re-layouts  19.5 us
    dynamic_slice x16, local copies, waits for them, and re-layouts, brick_step(): return lax.cond(own_flags[position] > 0, brick_compute, skip_brick, summed)  19.3 us
  transfers between devices with their start and end apart: 27, of which 12 were waited for; matrix products, arithmetic and copies ran while one was open for 2% of the time, Pallas kernels for 0%

profile of v1, /device:TPU:1, one launch (start us, length us, event | category | flops | bytes accessed | tf_op | source)
XLA Modules:
  0.0 934.0 jit_solution(12375417718896192266)
XLA Ops:
  1.4 4.5 collective-permute-start.3
  5.9 1.9 collective-permute-start.4
  12.2 8.5 collective-permute-done
  22.2 4.0 collective-permute-start.5
  27.7 3.0 collective-permute-done.6
  30.9 2.2 collective-permute-start.7
  34.4 3.4 collective-permute-start.2
  37.8 3.5 collective-permute-done.8
  41.9 4.7 fusion.62
  48.3 46.5 %while.51 = (s32[]{:T(128)}, f32[3,17,17,129]{3,2,1,0:T(8,128)}, s32[8]{0:T(128)}, f32[3,17,17,129]{3,2,1,0:T(8,128)S(1)}, f32[16,16,128]{2,1,0:T(8,128)}, /*index=5*/s32[]{:T(128)}, s32[1]{0:T(128)}) while((s32[]{:T(128)}, f32[3,17,17,129]{3,2,1,0:T(8,128)}, s32[8]{0:T(128)}, f32[3,17,17,129]{3,2,1,0:T(8,128)S(1)}, ...), condition=%wide.region_8.9_spmd.clone, body=%wide.region_5.8_spmd.sunk.clone.sunk | while | flops 28527780 | bytes 7407486 | solution.py:252
  55.8 31.4 %conditional.12 = (f32[3,17,17,129]{3,2,1,0:T(8,128)}) conditional(s32[]{:T(128)} %bitcast.53, f32[3,17,17,129]{3,2,1,0:T(8,128)} %get-tuple-element.762, (s32[]{:T(128)}, f32[3,17,17,129]{3,2,1,0:T(8,128)}, f32[3,17,17,129]{3,2,1,0:T(8,128)S(1)}, f32[16,16,128]{2,1,0:T(8,128)}) %tuple.222), branch_computations={%region_6.6_spmd, %region_7.7_spmd.clone} | conditional | flops 28527776 | bytes 7407351 | solution.py:250
  63.3 3.8 reshape.1039
  73.2 2.6 add_add_fusion
  75.8 11.4 %dynamic_update_slice.12 = f32[3,17,17,129]{3,2,1,0:T(8,128)} dynamic-update-slice(f32[3,17,17,129]{3,2,1,0:T(8,128)} %get-tuple-element.486, f32[3,17,17,17]{3,2,1,0:T(8,128)S(1)} %add_add_fusion, s32[]{:T(128)} %constant.166.clone.1, s32[]{:T(128)} %constant.166.clone.1, s32[]{:T(128)} %constant.166.clone.1, s32[]{:T(128)S(6)} %select_n.81) | dynamic-update-slice | bytes 117916 | tf_op jit(solution)/shard_map/while/body/eval_jaxpr/cond/branch_1_fun/dynamic_update_slice | solution.py:233
  95.7 163.3 %collective-permute-start.9 = (f32[3,1,17,129]{3,2,1,0:T(8,128)S(1)}, f32[3,1,17,129]{3,2,1,0:T(8,128)S(1)}, u32[]{:S(2)}, u32[]{:S(2)}) collective-permute-start(f32[3,1,17,129]{3,2,1,0:T(8,128)S(1)} %get-tuple-element.599), channel_id=1, source_target_pairs={{0,32},{32,64},{64,96},{96,128},{128,160},{160,192},{192,224},{1,3... | collective-permute-start | bytes 78956 | tf_op jit(solution)/shard_map/ppermute | solution.py:26
  259.1 54.8 %collective-permute-start.10 = (f32[3,1,17,129]{3,2,1,0:T(8,128)S(1)}, f32[3,1,17,129]{3,2,1,0:T(8,128)S(1)}, u32[]{:S(2)}, u32[]{:S(2)}) collective-permute-start(f32[3,1,17,129]{3,2,1,0:T(8,128)S(1)} %get-tuple-element.600), channel_id=1, source_target_pairs={{32,0},{64,32},{96,64},{128,96},{160,128},{192,160},{224,192},{33,... | collective-permute-start | bytes 78956 | tf_op jit(solution)/shard_map/ppermute | solution.py:29
  313.9 1.6 copy.46
  318.8 4.4 collective-permute-done.12
  324.4 1.6 copy.48
  326.1 21.4 %collective-permute-start.13 = (f32[3,19,19,1]{2,1,3,0:T(8,128)S(1)}, f32[3,19,19,1]{2,1,3,0:T(8,128)S(1)}, u32[]{:S(2)}, u32[]{:S(2)}) collective-permute-start(f32[3,19,19,1]{2,1,3,0:T(8,128)S(1)} %copy.48), channel_id=1, source_target_pairs={{0,1},{1,2},{2,3},{4,5},{5,6},{6,7},{8,9},{9,10},{10,11},{12,13},{... | collective-permute-start | bytes 13004 | tf_op jit(solution)/shard_map/ppermute | solution.py:26
  350.5 1.5 copy.51
  353.6 2.1 copy.52
  355.7 1.8 pad_maximum_fusion.1
  365.0 6.0 all-reduce.37
  373.6 1.4 dynamic-update-slice.1
  375.5 6.8 all-reduce.39
  386.7 12.4 %all-reduce.33 = (f32[8]{0:T(128)S(1)}, f32[8]{0:T(128)S(1)}) all-reduce(f32[8]{0:T(128)S(1)} %dynamic-update-slice.2, f32[8]{0:T(128)S(1)} %dynamic-update-slice.6), channel_id=1, replica_groups=mesh['gx_0'=4,'gx_1'=2,'gy'=8,'gz'=4] {'gy'}, use_global_device_ids=true, to_apply=%add.18 | all-reduce | flops 16 | bytes 128
  401.7 1.4 dynamic-update-slice.3
  403.1 6.0 all-reduce.35
  414.3 46.4 %while.52 = (s32[]{:T(128)}, f32[3,17,17,129]{3,2,1,0:T(8,128)}, s32[8]{0:T(128)}, f32[3,17,17,129]{3,2,1,0:T(8,128)S(1)}, f32[16,16,128]{2,1,0:T(8,128)}, /*index=5*/s32[]{:T(128)}, s32[1]{0:T(128)}) while((s32[]{:T(128)}, f32[3,17,17,129]{3,2,1,0:T(8,128)}, s32[8]{0:T(128)}, f32[3,17,17,129]{3,2,1,0:T(8,128)S(1)}, ...), condition=%wide.region_22.23_spmd.clone, body=%wide.region_19.22_spmd.sunk.clone.sunk | while | flops 28527780 | bytes 7407486 | solution.py:252
  421.8 31.3 %conditional.13 = (f32[3,17,17,129]{3,2,1,0:T(8,128)}) conditional(s32[]{:T(128)} %bitcast.54, f32[3,17,17,129]{3,2,1,0:T(8,128)} %get-tuple-element.783, (s32[]{:T(128)}, f32[3,17,17,129]{3,2,1,0:T(8,128)}, f32[3,17,17,129]{3,2,1,0:T(8,128)S(1)}, f32[16,16,128]{2,1,0:T(8,128)}) %tuple.224), branch_computations={%region_20.20_spmd, %region_21.21_spmd.clone} | conditional | flops 28527776 | bytes 7407351 | solution.py:250
  429.3 3.8 reshape.1040
  439.1 2.6 add_add_fusion.1
  441.7 11.4 %dynamic_update_slice.13 = f32[3,17,17,129]{3,2,1,0:T(8,128)} dynamic-update-slice(f32[3,17,17,129]{3,2,1,0:T(8,128)} %get-tuple-element.494, f32[3,17,17,17]{3,2,1,0:T(8,128)S(1)} %add_add_fusion.1, s32[]{:T(128)} %constant.174.clone.1, s32[]{:T(128)} %constant.174.clone.1, s32[]{:T(128)} %constant.174.clone.1, s32[]{:T(128)S(6)} %select_n.83) | dynamic-update-slice | bytes 117916 | tf_op jit(solution)/shard_map/while/body/eval_jaxpr/cond/branch_1_fun/dynamic_update_slice | solution.py:233
  461.7 165.3 %collective-permute-start.15 = (f32[3,1,17,129]{3,2,1,0:T(8,128)S(1)}, f32[3,1,17,129]{3,2,1,0:T(8,128)S(1)}, u32[]{:S(2)}, u32[]{:S(2)}) collective-permute-start(f32[3,1,17,129]{3,2,1,0:T(8,128)S(1)} %get-tuple-element.593), channel_id=1, source_target_pairs={{0,32},{32,64},{64,96},{96,128},{128,160},{160,192},{192,224},{1,3... | collective-permute-start | bytes 78956 | tf_op jit(solution)/shard_map/ppermute | solution.py:26
  627.0 56.4 %collective-permute-start.16 = (f32[3,1,17,129]{3,2,1,0:T(8,128)S(1)}, f32[3,1,17,129]{3,2,1,0:T(8,128)S(1)}, u32[]{:S(2)}, u32[]{:S(2)}) collective-permute-start(f32[3,1,17,129]{3,2,1,0:T(8,128)S(1)} %get-tuple-element.594), channel_id=1, source_target_pairs={{32,0},{64,32},{96,64},{128,96},{160,128},{192,160},{224,192},{33,... | collective-permute-start | bytes 78956 | tf_op jit(solution)/shard_map/ppermute | solution.py:29
  683.4 1.6 copy.54
  688.3 4.4 collective-permute-done.18
  694.0 1.6 copy.56
  695.6 5.0 collective-permute-start.19
  701.7 1.5 collective-permute-start.20
  703.2 1.6 slice.1586
  704.7 1.5 copy.59
  706.7 2.1 copy.60
  708.8 1.8 pad_maximum_fusion.3
  716.4 6.7 all-reduce.36
  727.0 6.4 all-reduce.38
  737.2 12.1 %all-reduce.32 = (f32[8]{0:T(128)S(1)}, f32[8]{0:T(128)S(1)}) all-reduce(f32[8]{0:T(128)S(1)} %dynamic-update-slice.10, f32[8]{0:T(128)S(1)} %dynamic-update-slice.14), channel_id=1, replica_groups=mesh['gx_0'=4,'gx_1'=2,'gy'=8,'gz'=4] {'gy'}, use_global_device_ids=true, to_apply=%add.26 | all-reduce | flops 16 | bytes 128
  749.9 1.4 dynamic-update-slice.15
  751.9 1.4 dynamic-update-slice.11
  753.3 8.0 all-reduce.34
  767.1 1.4 multiply_add_fusion
  768.8 29.5 %while.53 = (s32[]{:T(128)}, f32[16,16,128]{2,1,0:T(8,128)S(1)}, s32[8]{0:T(128)}, f32[3,17,17,129]{3,2,1,0:T(8,128)S(1)}, s32[]{:T(128)}, /*index=5*/s32[1]{0:T(128)}) while((s32[]{:T(128)}, f32[16,16,128]{2,1,0:T(8,128)S(1)}, s32[8]{0:T(128)}, f32[3,17,17,129]{3,2,1,0:T(8,128)S(1)}, s32[]{:T(128)}, ...), condition=%wide.region_32.33_spmd.clone, body=%wide.region_28.32_spmd.sunk.clone.sunk | while | flops 28504076 | bytes 4812342 | solution.py:301
  776.4 14.4 %conditional.14 = (f32[16,16,128]{2,1,0:T(8,128)S(1)}) conditional(s32[]{:T(128)} %bitcast.55, f32[16,16,128]{2,1,0:T(8,128)S(1)} %get-tuple-element.803, (s32[]{:T(128)}, f32[3,17,17,129]{3,2,1,0:T(8,128)S(1)}, f32[16,16,128]{2,1,0:T(8,128)S(1)}) %tuple.226), branch_computations={%region_29.29_spmd, %region_30.31_spmd.clone} | conditional | flops 28504072 | bytes 4812223 | solution.py:299
  783.8 3.8 reshape.1041
  788.3 2.5 dynamic_update_slice.14
  798.6 1.7 fusion.65
  800.3 81.5 %collective-permute-start.21 = (f32[2,16,128]{2,1,0:T(8,128)S(1)}, f32[2,16,128]{2,1,0:T(8,128)S(1)}, u32[]{:S(2)}, u32[]{:S(2)}) collective-permute-start(f32[2,16,128]{2,1,0:T(8,128)S(1)} %get-tuple-element.615), channel_id=1, source_target_pairs={{0,32},{32,64},{64,96},{96,128},{128,160},{160,192},{192,224},{1,3... | collective-permute-start | bytes 49160 | tf_op jit(solution)/shard_map/ppermute | solution.py:26
  881.8 26.3 %collective-permute-start.22 = (f32[2,16,128]{2,1,0:T(8,128)S(1)}, f32[2,16,128]{2,1,0:T(8,128)S(1)}, u32[]{:S(2)}, u32[]{:S(2)}) collective-permute-start(f32[2,16,128]{2,1,0:T(8,128)S(1)} %get-tuple-element.616), channel_id=1, source_target_pairs={{32,0},{64,32},{96,64},{128,96},{160,128},{192,160},{224,192},{33,... | collective-permute-start | bytes 49160 | tf_op jit(solution)/shard_map/ppermute | solution.py:29
  912.3 2.4 collective-permute-done.24
  915.0 5.7 collective-permute-start.25
  922.0 4.0 collective-permute-done.25
  926.1 4.3 collective-permute-done.26
  930.7 2.9 fusion.189
  (398 shorter events, 135.8 us)
Async XLA Ops:
  1.4 20.7 %collective-permute-start.3 = (f32[2,16,128]{2,1,0:T(8,128)S(1)}, f32[2,16,128]{2,1,0:T(8,128)S(1)}, u32[]{:S(2)}, u32[]{:S(2)}) collective-permute-start(f32[2,16,128]{2,1,0:T(8,128)S(1)} %get-tuple-element.621), channel_id=1, source_target_pairs={{0,32},{32,64},{64,96},{96,128},{128,160},{160,192},{192,224},{1,3... | collective-permute-start | bytes 49160 | tf_op jit(solution)/shard_map/ppermute | solution.py:26
  5.9 16.3 %collective-permute-start.4 = (f32[2,16,128]{2,1,0:T(8,128)S(1)}, f32[2,16,128]{2,1,0:T(8,128)S(1)}, u32[]{:S(2)}, u32[]{:S(2)}) collective-permute-start(f32[2,16,128]{2,1,0:T(8,128)S(1)} %get-tuple-element.620), channel_id=1, source_target_pairs={{32,0},{64,32},{96,64},{128,96},{160,128},{192,160},{224,192},{33,... | collective-permute-start | bytes 49160 | tf_op jit(solution)/shard_map/ppermute | solution.py:29
  7.8 12.9 %collective-permute-start = (f32[3,16,16,1]{3,2,1,0:T(8,128)}, f32[3,16,16,1]{3,2,1,0:T(8,128)S(1)}, u32[]{:S(2)}, u32[]{:S(2)}) collective-permute-start(f32[3,16,16,1]{3,2,1,0:T(8,128)} %bitcast.56), channel_id=1, source_target_pairs={{1,0},{2,1},{3,2},{5,4},{6,5},{7,6},{9,8},{10,9},{11,10},{13,12},{... | collective-permute-start | bytes 9224 | tf_op jit(solution)/shard_map/ppermute | solution.py:37
  9.2 32.5 %copy-start.59 = (f32[128]{0:T(128)}, f32[128]{0:T(128)S(1)}, u32[]{:S(2)}) copy-start(f32[128]{0:T(128)S(1)} %get-tuple-element.663) | copy-start | bytes 1540
  9.2 32.5 %copy-start.61 = (f32[128]{0:T(128)}, f32[128]{0:T(128)S(1)}, u32[]{:S(2)}) copy-start(f32[128]{0:T(128)S(1)} %get-tuple-element.664) | copy-start | bytes 1540
  9.2 32.4 %copy-start.63 = (f32[128]{0:T(128)}, f32[128]{0:T(128)S(1)}, u32[]{:S(2)}) copy-start(f32[128]{0:T(128)S(1)} %get-tuple-element.665) | copy-start | bytes 1540
  9.2 32.4 %copy-start.65 = (f32[128]{0:T(128)}, f32[128]{0:T(128)S(1)}, u32[]{:S(2)}) copy-start(f32[128]{0:T(128)S(1)} %get-tuple-element.666) | copy-start | bytes 1540
  10.6 36.0 %copy-start.7 = (f32[17,17,129]{2,1,0:T(8,128)}, f32[17,17,129]{2,1,0:T(8,128)S(1)}, u32[]{:S(2)}) copy-start(f32[17,17,129]{2,1,0:T(8,128)S(1)} %broadcast_multiply_fusion) | copy-start | bytes 447376
  10.7 31.0 %copy-start.21 = (f32[16,16]{1,0:T(8,128)}, f32[16,16]{1,0:T(8,128)S(1)}, u32[]{:S(2)}) copy-start(f32[16,16]{1,0:T(8,128)S(1)} %get-tuple-element.632) | copy-start | bytes 3076
  10.7 31.0 %copy-start.23 = (f32[16,16]{1,0:T(8,128)}, f32[16,16]{1,0:T(8,128)S(1)}, u32[]{:S(2)}) copy-start(f32[16,16]{1,0:T(8,128)S(1)} %get-tuple-element.633) | copy-start | bytes 3076
  10.7 31.0 %copy-start.25 = (f32[16,16]{1,0:T(8,128)}, f32[16,16]{1,0:T(8,128)S(1)}, u32[]{:S(2)}) copy-start(f32[16,16]{1,0:T(8,128)S(1)} %get-tuple-element.634) | copy-start | bytes 3076
  10.7 31.0 %copy-start.27 = (f32[16,16]{1,0:T(8,128)}, f32[16,16]{1,0:T(8,128)S(1)}, u32[]{:S(2)}) copy-start(f32[16,16]{1,0:T(8,128)S(1)} %get-tuple-element.635) | copy-start | bytes 3076
  10.7 31.0 %copy-start.29 = (f32[16,16]{1,0:T(8,128)}, f32[16,16]{1,0:T(8,128)S(1)}, u32[]{:S(2)}) copy-start(f32[16,16]{1,0:T(8,128)S(1)} %get-tuple-element.636) | copy-start | bytes 3076
  10.8 31.0 %copy-start.31 = (f32[16,16]{1,0:T(8,128)}, f32[16,16]{1,0:T(8,128)S(1)}, u32[]{:S(2)}) copy-start(f32[16,16]{1,0:T(8,128)S(1)} %get-tuple-element.637) | copy-start | bytes 3076
  10.8 31.0 %copy-start.33 = (f32[16,16]{1,0:T(8,128)}, f32[16,16]{1,0:T(8,128)S(1)}, u32[]{:S(2)}) copy-start(f32[16,16]{1,0:T(8,128)S(1)} %get-tuple-element.638) | copy-start | bytes 3076
  10.8 31.0 %copy-start.35 = (f32[16,16]{1,0:T(8,128)}, f32[16,16]{1,0:T(8,128)S(1)}, u32[]{:S(2)}) copy-start(f32[16,16]{1,0:T(8,128)S(1)} %get-tuple-element.639) | copy-start | bytes 3076
  10.8 31.0 %copy-start.37 = (f32[16,16]{1,0:T(8,128)}, f32[16,16]{1,0:T(8,128)S(1)}, u32[]{:S(2)}) copy-start(f32[16,16]{1,0:T(8,128)S(1)} %get-tuple-element.640) | copy-start | bytes 3076
  10.8 31.0 %copy-start.39 = (f32[16,16]{1,0:T(8,128)}, f32[16,16]{1,0:T(8,128)S(1)}, u32[]{:S(2)}) copy-start(f32[16,16]{1,0:T(8,128)S(1)} %get-tuple-element.641) | copy-start | bytes 3076
  10.8 31.0 %copy-start.41 = (f32[16,16]{1,0:T(8,128)}, f32[16,16]{1,0:T(8,128)S(1)}, u32[]{:S(2)}) copy-start(f32[16,16]{1,0:T(8,128)S(1)} %get-tuple-element.642) | copy-start | bytes 3076
  10.8 31.0 %copy-start.43 = (f32[16,16]{1,0:T(8,128)}, f32[16,16]{1,0:T(8,128)S(1)}, u32[]{:S(2)}) copy-start(f32[16,16]{1,0:T(8,128)S(1)} %get-tuple-element.643) | copy-start | bytes 3076
  10.8 31.0 %copy-start.45 = (f32[16,16]{1,0:T(8,128)}, f32[16,16]{1,0:T(8,128)S(1)}, u32[]{:S(2)}) copy-start(f32[16,16]{1,0:T(8,128)S(1)} %get-tuple-element.644) | copy-start | bytes 3076
  10.8 31.0 %copy-start.47 = (f32[16,16]{1,0:T(8,128)}, f32[16,16]{1,0:T(8,128)S(1)}, u32[]{:S(2)}) copy-start(f32[16,16]{1,0:T(8,128)S(1)} %get-tuple-element.645) | copy-start | bytes 3076
  10.8 31.0 %copy-start.49 = (f32[16,16]{1,0:T(8,128)}, f32[16,16]{1,0:T(8,128)S(1)}, u32[]{:S(2)}) copy-start(f32[16,16]{1,0:T(8,128)S(1)} %get-tuple-element.646) | copy-start | bytes 3076
  10.9 31.0 %copy-start.51 = (f32[16,16]{1,0:T(8,128)}, f32[16,16]{1,0:T(8,128)S(1)}, u32[]{:S(2)}) copy-start(f32[16,16]{1,0:T(8,128)S(1)} %get-tuple-element.647) | copy-start | bytes 3076
  10.9 31.0 %copy-start.53 = (f32[16,16]{1,0:T(8,128)}, f32[16,16]{1,0:T(8,128)S(1)}, u32[]{:S(2)}) copy-start(f32[16,16]{1,0:T(8,128)S(1)} %get-tuple-element.648) | copy-start | bytes 3076
  10.9 31.0 %copy-start.55 = (f32[16,16]{1,0:T(8,128)}, f32[16,16]{1,0:T(8,128)S(1)}, u32[]{:S(2)}) copy-start(f32[16,16]{1,0:T(8,128)S(1)} %get-tuple-element.649) | copy-start | bytes 3076
  10.9 31.0 %copy-start.57 = (f32[16,16]{1,0:T(8,128)}, f32[16,16]{1,0:T(8,128)S(1)}, u32[]{:S(2)}) copy-start(f32[16,16]{1,0:T(8,128)S(1)} %get-tuple-element.650) | copy-start | bytes 3076
  20.8 6.9 collective-permute-start.1
  22.2 5.5 collective-permute-start.5
  26.2 4.5 collective-permute-start.6
  30.9 6.9 collective-permute-start.7
  33.1 8.2 collective-permute-start.8
  34.4 12.1 %collective-permute-start.2 = (f32[3,1,17,129]{3,2,1,0:T(8,128)S(1)}, f32[3,1,17,129]{3,2,1,0:T(8,128)S(1)}, u32[]{:S(2)}, u32[]{:S(2)}) collective-permute-start(f32[3,1,17,129]{3,2,1,0:T(8,128)S(1)} %pad_maximum_fusion.25), channel_id=1, source_target_pairs={{32,0},{64,32},{96,64},{128,96},{160,128},{192,160},{224,192},{33,... | collective-permute-start | bytes 78956 | tf_op jit(solution)/shard_map/ppermute | solution.py:37
  95.7 219.8 %collective-permute-start.9 = (f32[3,1,17,129]{3,2,1,0:T(8,128)S(1)}, f32[3,1,17,129]{3,2,1,0:T(8,128)S(1)}, u32[]{:S(2)}, u32[]{:S(2)}) collective-permute-start(f32[3,1,17,129]{3,2,1,0:T(8,128)S(1)} %get-tuple-element.599), channel_id=1, source_target_pairs={{0,32},{32,64},{64,96},{96,128},{128,160},{160,192},{192,224},{1,3... | collective-permute-start | bytes 78956 | tf_op jit(solution)/shard_map/ppermute | solution.py:26
  259.1 56.5 %collective-permute-start.10 = (f32[3,1,17,129]{3,2,1,0:T(8,128)S(1)}, f32[3,1,17,129]{3,2,1,0:T(8,128)S(1)}, u32[]{:S(2)}, u32[]{:S(2)}) collective-permute-start(f32[3,1,17,129]{3,2,1,0:T(8,128)S(1)} %get-tuple-element.600), channel_id=1, source_target_pairs={{32,0},{64,32},{96,64},{128,96},{160,128},{192,160},{224,192},{33,... | collective-permute-start | bytes 78956 | tf_op jit(solution)/shard_map/ppermute | solution.py:29
  315.7 3.1 collective-permute-start.11
  317.0 6.2 collective-permute-start.12
  326.1 25.9 %collective-permute-start.13 = (f32[3,19,19,1]{2,1,3,0:T(8,128)S(1)}, f32[3,19,19,1]{2,1,3,0:T(8,128)S(1)}, u32[]{:S(2)}, u32[]{:S(2)}) collective-permute-start(f32[3,19,19,1]{2,1,3,0:T(8,128)S(1)} %copy.48), channel_id=1, source_target_pairs={{0,1},{1,2},{2,3},{4,5},{5,6},{6,7},{8,9},{9,10},{10,11},{12,13},{... | collective-permute-start | bytes 13004 | tf_op jit(solution)/shard_map/ppermute | solution.py:26
  348.6 5.0 collective-permute-start.14
  360.8 52.3 %copy-start.3 = (f32[3,17,17,129]{3,2,1,0:T(8,128)}, f32[3,17,17,129]{3,2,1,0:T(8,128)S(1)}, u32[]{:S(2)}) copy-start(f32[3,17,17,129]{3,2,1,0:T(8,128)S(1)} %fusion.6) | copy-start | bytes 1342120
  461.7 223.4 %collective-permute-start.15 = (f32[3,1,17,129]{3,2,1,0:T(8,128)S(1)}, f32[3,1,17,129]{3,2,1,0:T(8,128)S(1)}, u32[]{:S(2)}, u32[]{:S(2)}) collective-permute-start(f32[3,1,17,129]{3,2,1,0:T(8,128)S(1)} %get-tuple-element.593), channel_id=1, source_target_pairs={{0,32},{32,64},{64,96},{96,128},{128,160},{160,192},{192,224},{1,3... | collective-permute-start | bytes 78956 | tf_op jit(solution)/shard_map/ppermute | solution.py:26
  627.0 58.1 %collective-permute-start.16 = (f32[3,1,17,129]{3,2,1,0:T(8,128)S(1)}, f32[3,1,17,129]{3,2,1,0:T(8,128)S(1)}, u32[]{:S(2)}, u32[]{:S(2)}) collective-permute-start(f32[3,1,17,129]{3,2,1,0:T(8,128)S(1)} %get-tuple-element.594), channel_id=1, source_target_pairs={{32,0},{64,32},{96,64},{128,96},{160,128},{192,160},{224,192},{33,... | collective-permute-start | bytes 78956 | tf_op jit(solution)/shard_map/ppermute | solution.py:29
  685.2 3.1 collective-permute-start.17
  686.5 6.2 collective-permute-start.18
  695.6 10.6 %collective-permute-start.19 = (f32[3,19,19,1]{2,1,3,0:T(8,128)S(1)}, f32[3,19,19,1]{2,1,3,0:T(8,128)S(1)}, u32[]{:S(2)}, u32[]{:S(2)}) collective-permute-start(f32[3,19,19,1]{2,1,3,0:T(8,128)S(1)} %copy.56), channel_id=1, source_target_pairs={{0,1},{1,2},{2,3},{4,5},{5,6},{6,7},{8,9},{9,10},{10,11},{12,13},{... | collective-permute-start | bytes 13004 | tf_op jit(solution)/shard_map/ppermute | solution.py:26
  701.7 5.0 collective-permute-start.20
  713.0 54.1 %copy-start.2 = (f32[3,16,16,129]{3,2,1,0:T(8,128)S(1)}, f32[3,16,16,129]{3,2,1,0:T(8,128)}, u32[]{:S(2)}) copy-start(f32[3,16,16,129]{3,2,1,0:T(8,128)} %copy-done) | copy-start | bytes 1188868
  713.0 54.1 %copy-start.4 = (f32[3,17,17,129]{3,2,1,0:T(8,128)S(1)}, f32[3,17,17,129]{3,2,1,0:T(8,128)}, u32[]{:S(2)}) copy-start(f32[3,17,17,129]{3,2,1,0:T(8,128)} %copy-done.3) | copy-start | bytes 1342120
  713.0 54.1 %copy-start.13 = (f32[3,1,17,129]{3,2,1,0:T(8,128)S(1)}, f32[3,1,17,129]{3,2,1,0:T(8,128)}, u32[]{:S(2)}) copy-start(f32[3,1,17,129]{3,2,1,0:T(8,128)} %copy-done.11) | copy-start | bytes 78952
  768.5 29.8 %copy-start.15 = (f32[16,16,128]{2,1,0:T(8,128)S(1)}, f32[16,16,128]{2,1,0:T(8,128)}, u32[]{:S(2)}) copy-start(f32[16,16,128]{2,1,0:T(8,128)} %get-tuple-element.557) | copy-start | bytes 393220
  768.6 29.8 %copy-start.16 = (f32[16,16,128]{2,1,0:T(8,128)S(1)}, f32[16,16,128]{2,1,0:T(8,128)}, u32[]{:S(2)}) copy-start(f32[16,16,128]{2,1,0:T(8,128)} %get-tuple-element.558) | copy-start | bytes 393220
  768.6 29.8 %copy-start.22 = (f32[16,16]{1,0:T(8,128)S(1)}, f32[16,16]{1,0:T(8,128)}, u32[]{:S(2)}) copy-start(f32[16,16]{1,0:T(8,128)} %copy-done.21) | copy-start | bytes 3076
  768.6 29.8 %copy-start.24 = (f32[16,16]{1,0:T(8,128)S(1)}, f32[16,16]{1,0:T(8,128)}, u32[]{:S(2)}) copy-start(f32[16,16]{1,0:T(8,128)} %copy-done.23) | copy-start | bytes 3076
  768.6 29.8 %copy-start.26 = (f32[16,16]{1,0:T(8,128)S(1)}, f32[16,16]{1,0:T(8,128)}, u32[]{:S(2)}) copy-start(f32[16,16]{1,0:T(8,128)} %copy-done.25) | copy-start | bytes 3076
  768.6 29.8 %copy-start.28 = (f32[16,16]{1,0:T(8,128)S(1)}, f32[16,16]{1,0:T(8,128)}, u32[]{:S(2)}) copy-start(f32[16,16]{1,0:T(8,128)} %copy-done.27) | copy-start | bytes 3076
  768.6 29.8 %copy-start.30 = (f32[16,16]{1,0:T(8,128)S(1)}, f32[16,16]{1,0:T(8,128)}, u32[]{:S(2)}) copy-start(f32[16,16]{1,0:T(8,128)} %copy-done.29) | copy-start | bytes 3076
  768.6 29.8 %copy-start.32 = (f32[16,16]{1,0:T(8,128)S(1)}, f32[16,16]{1,0:T(8,128)}, u32[]{:S(2)}) copy-start(f32[16,16]{1,0:T(8,128)} %copy-done.31) | copy-start | bytes 3076
  768.6 29.8 %copy-start.34 = (f32[16,16]{1,0:T(8,128)S(1)}, f32[16,16]{1,0:T(8,128)}, u32[]{:S(2)}) copy-start(f32[16,16]{1,0:T(8,128)} %copy-done.33) | copy-start | bytes 3076
  800.3 107.8 %collective-permute-start.21 = (f32[2,16,128]{2,1,0:T(8,128)S(1)}, f32[2,16,128]{2,1,0:T(8,128)S(1)}, u32[]{:S(2)}, u32[]{:S(2)}) collective-permute-start(f32[2,16,128]{2,1,0:T(8,128)S(1)} %get-tuple-element.615), channel_id=1, source_target_pairs={{0,32},{32,64},{64,96},{96,128},{128,160},{160,192},{192,224},{1,3... | collective-permute-start | bytes 49160 | tf_op jit(solution)/shard_map/ppermute | solution.py:26
  881.8 27.1 %collective-permute-start.22 = (f32[2,16,128]{2,1,0:T(8,128)S(1)}, f32[2,16,128]{2,1,0:T(8,128)S(1)}, u32[]{:S(2)}, u32[]{:S(2)}) collective-permute-start(f32[2,16,128]{2,1,0:T(8,128)S(1)} %get-tuple-element.616), channel_id=1, source_target_pairs={{32,0},{64,32},{96,64},{128,96},{160,128},{192,160},{224,192},{33,... | collective-permute-start | bytes 49160 | tf_op jit(solution)/shard_map/ppermute | solution.py:29
  909.0 3.4 collective-permute-start.23
  910.3 4.5 collective-permute-start.24
  915.0 11.1 %collective-permute-start.25 = (f32[20,20,2]{2,1,0:T(8,128)S(1)}, f32[20,20,2]{2,1,0:T(8,128)S(1)}, u32[]{:S(2)}, u32[]{:S(2)}) collective-permute-start(f32[20,20,2]{2,1,0:T(8,128)S(1)} %get-tuple-element.601), channel_id=1, source_target_pairs={{0,1},{1,2},{2,3},{4,5},{5,6},{6,7},{8,9},{9,10},{10,11},{12,13},{... | collective-permute-start | bytes 9608 | tf_op jit(solution)/shard_map/ppermute | solution.py:26
  920.7 9.7 %collective-permute-start.26 = (f32[20,20,2]{2,1,0:T(8,128)S(1)}, f32[20,20,2]{2,1,0:T(8,128)S(1)}, u32[]{:S(2)}, u32[]{:S(2)}) collective-permute-start(f32[20,20,2]{2,1,0:T(8,128)S(1)} %get-tuple-element.602), channel_id=1, source_target_pairs={{1,0},{2,1},{3,2},{5,4},{6,5},{7,6},{9,8},{10,9},{11,10},{13,12},{... | collective-permute-start | bytes 9608 | tf_op jit(solution)/shard_map/ppermute | solution.py:29
  (36 other events, 658.5 us)
